TPU v7x, 32 devices: a whole 2x2x4 slice. The times are simulated.
32 devices in a mesh: span: 16 (over z, x, core), seq: 2 (over y).
Axes of the slice: x: 2, y: 2, z: 4, core: 2. Of those that a mesh axis runs over, the one named last changes fastest.
Arguments:
- tokens: bfloat16 [8192, 1024], P(('span', 'seq')), may hold values from -48 to 48
- w_qkv: bfloat16 [1024, 3072], P('span'), may hold values from -0.1875 to 0.1875
- w_out: bfloat16 [1024, 1024], replicated, may hold values from -0.1875 to 0.1875
- w_cross: bfloat16 [1024, 2048], replicated, may hold values from -0.1875 to 0.1875
- ln_gain: float32 [1024], replicated, may hold values from 0.5 to 1.5
- ln_bias: float32 [1024], replicated, may hold values from -3 to 3
- queries: bfloat16 [1024, 1024], replicated, may hold values from -144 to 144
Outputs:
- encoded: bfloat16 [8192, 1024], P(('span', 'seq'))
- cross_out: bfloat16 [1024, 1024], P('span')
All inputs are finite; a program needn't handle non-finite values.
Results may differ from a plain program's by a relative error of at most 0.013.
The roundings to bfloat16 on the way count: a program that leaves them out, or rounds other values in their place, can miss the bound.
Values may be sent and summed in bfloat16 or wider, within the bound.
A program may use at most 128 MiB of HBM per device.

v0:
```python
import jax
import jax.numpy as jnp
from jax import lax
from jax.sharding import PartitionSpec as P

H = 16
DH = 64
score_scale = 0.125


def layer_norm(residual, ln_gain, ln_bias):
    center = residual - jnp.mean(residual, -1, keepdims=True)
    spread = jnp.mean(center * center, -1, keepdims=True)
    return center * lax.rsqrt(spread + 1e-05) * ln_gain + ln_bias


def per_device(tokens, w_qkv, w_out, w_cross, ln_gain, ln_bias, queries):
    tok_rows = tokens.shape[0]
    model_width = tokens.shape[1]
    seq_count = lax.axis_size("seq")
    span_count = lax.axis_size("span")
    projected = jnp.dot(
        tokens,
        lax.all_gather(w_qkv, "span", axis=0, tiled=True),
        preferred_element_type=jnp.float32,
    )
    projected = projected.astype(jnp.bfloat16).reshape(tok_rows, 3, model_width)
    grouped = lax.all_to_all(projected, "seq", split_axis=2, concat_axis=0, tiled=True)
    span_length = tok_rows * seq_count
    heads_here = grouped.shape[2] // DH
    query_all = grouped[:, 0].reshape(span_length, heads_here, DH)
    key_all = grouped[:, 1].reshape(span_length, heads_here, DH)
    value_all = grouped[:, 2].reshape(span_length, heads_here, DH)
    block_rows = min(512, span_length)
    query_blocks = query_all.reshape(span_length // block_rows, block_rows, heads_here, DH)

    def attend(query_block):
        scores = (
            jnp.einsum("qhd,khd->hqk", query_block, key_all, preferred_element_type=jnp.float32)
            * score_scale
        )
        peaks = jnp.max(scores, -1, keepdims=True)
        powers = jnp.exp(scores - peaks)
        totals = jnp.sum(powers, -1, keepdims=True)
        mixed = jnp.einsum(
            "hqk,khd->qhd",
            powers.astype(jnp.bfloat16),
            value_all,
            preferred_element_type=jnp.float32,
        )
        mixed = mixed / jnp.transpose(totals, (1, 0, 2))
        return mixed.astype(jnp.bfloat16).reshape(block_rows, heads_here * DH)

    attn = lax.map(attend, query_blocks).reshape(span_length, heads_here * DH)
    attn_tokens = lax.all_to_all(attn, "seq", split_axis=0, concat_axis=1, tiled=True)
    residual = tokens.astype(jnp.float32) + jnp.dot(
        attn_tokens, w_out, preferred_element_type=jnp.float32
    )
    encoded = layer_norm(residual, ln_gain, ln_bias).astype(jnp.bfloat16)
    cross_kv = jnp.dot(encoded, w_cross, preferred_element_type=jnp.float32).astype(jnp.bfloat16)
    cross_keys = cross_kv[:, :model_width].reshape(tok_rows, H, DH)
    cross_values = cross_kv[:, model_width:].reshape(tok_rows, H, DH)
    query_count = queries.shape[0]
    query_heads = queries.reshape(query_count, H, DH)
    cross_scores = (
        jnp.einsum("qhd,khd->qhk", query_heads, cross_keys, preferred_element_type=jnp.float32)
        * score_scale
    )
    local_peak = jnp.max(cross_scores, -1)
    cross_peak = lax.pmax(local_peak, ("span", "seq"))
    cross_powers = jnp.exp(cross_scores - cross_peak[:, :, None])
    cross_total = jnp.sum(cross_powers, -1)
    numerator = jnp.einsum(
        "qhk,khd->qhd",
        cross_powers.astype(jnp.bfloat16),
        cross_values,
        preferred_element_type=jnp.float32,
    )
    numerator = numerator.reshape(query_count, model_width)
    own_rows = query_count // span_count
    summed, sum_total = lax.psum((numerator, cross_total), ("span", "seq"))
    row_start = lax.axis_index("span") * own_rows
    summed = lax.dynamic_slice_in_dim(summed, row_start, own_rows, 0)
    sum_total = lax.dynamic_slice_in_dim(sum_total, row_start, own_rows, 0)
    cross_out = summed.reshape(own_rows, H, DH) / sum_total[:, :, None]
    return (encoded, cross_out.reshape(own_rows, model_width).astype(jnp.bfloat16))


def solution(mesh):
    in_specs = (P(("span", "seq"), None), P("span", None), P(), P(), P(), P(), P())
    out_specs = (P(("span", "seq"), None), P("span", None))
    return jax.shard_map(
        per_device, mesh=mesh, in_specs=in_specs, out_specs=out_specs, check_vma=False
    )
```

profile of v0, /device:TPU:0, one launch (start us, length us, event | category | flops | bytes accessed | tf_op | source)
XLA Modules:
  0.0 455.3 jit_solution(16979895533489003373)
XLA Ops:
  7.2 0.7 all-gather.2.cloned.1.call-update
  7.9 66.5 %all-gather.2.cloned.1.call-done = bf16[1024,3072]{1,0:T(8,128)(2,1)} async-done(((bf16[64,3072]{1,0:T(8,128)(2,1)}), bf16[1024,3072]{1,0:T(8,128)(2,1)}) %all-gather.2.cloned.1.call-update) | async-done | bytes 6291472 | tf_op jit(solution)/shard_map/all_gather | solution.py:24
  74.4 5.9 %convolution_convert_fusion = bf16[256,3072]{1,0:T(8,128)(2,1)} fusion(bf16[256,1024]{1,0:T(8,128)(2,1)} %param.7, bf16[1024,3072]{1,0:T(8,128)(2,1)} %all-gather.2.cloned.1.call-done), kind=kOutput, calls=%fused_computation.15 | convolution fusion | flops 1611399168 | bytes 8388608 | tf_op jit(solution)/shard_map/dot_general | solution.py:22
  80.3 2.6 copy.36
  82.9 2.8 copy.37
  85.7 28.1 %all_to_all.37 = bf16[256,3,1024]{0,1,2:T(4,128)(2,1)S(1)} all-to-all(bf16[256,3,1024]{0,1,2:T(4,128)(2,1)S(1)} %copy.37), channel_id=1, replica_groups=mesh['span'=16,'seq'=2] {'seq'}, dimensions={2} | all-to-all | bytes 3145728 | tf_op jit(solution)/shard_map/all_to_all | solution.py:28
  113.8 1.4 copy.38
  115.1 2.6 copy.39
  117.8 2.3 fusion.20
  120.0 1.0 copy.40
  121.2 1.3 copy.42
  122.5 1.3 multiply_reduce_fusion
  123.8 1.4 fusion.7
  125.2 2.4 divide_convert_fusion
  127.6 1.2 all_to_all.31
  128.8 0.9 copy.44
  129.7 3.5 all-to-all-start.1
  133.4 4.0 copy.47
  137.4 3.6 all-to-all-done.1
  141.0 0.8 fusion.22
  141.8 0.3 multiply_reduce_fusion.1
  142.4 3.7 convolution_convert_fusion.1
  146.0 0.9 fusion.21
  146.9 1.2 copy.46
  148.1 10.3 %bitcast_reduce_fusion = (f32[1024,16]{0,1:T(8,128)}, f32[16,256,1024]{2,1,0:T(8,128)}) fusion(bf16[256,16,64]{0,2,1:T(8,128)(2,1)S(1)} %bitcast.58, bf16[1024,16,64]{0,2,1:T(8,128)(2,1)} %bitcast.51), kind=kOutput, calls=%fused_computation.1 | convolution fusion | flops 545243136 | bytes 19464192 | tf_op jit(solution)/shard_map/qhd,khd->qhk/dot_general | solution.py:66
  158.7 117.2 %all-reduce.4.cloned.1.call-done = f32[1024,16]{0,1:T(8,128)} async-done(((f32[1024,16]{0,1:T(8,128)}), f32[1024,16]{0,1:T(8,128)}) %all-reduce.4.cloned.1.call-update) | async-done | bytes 65552 | tf_op jit(solution)/shard_map/pmax | solution.py:70
  276.0 10.7 %fusion.3 = f32[16,64,1024]{2,1,0:T(8,128)} fusion(bf16[256,16,64]{0,2,1:T(8,128)(2,1)S(1)} %bitcast.59, f32[16,256,1024]{2,1,0:T(8,128)} %get-tuple-element.29, f32[1024,16]{0,1:T(8,128)} %all-reduce.4.cloned.1.call-done), kind=kOutput, calls=%fused_computation.5 | convolution fusion | flops 549453824 | bytes 21561344 | tf_op jit(solution)/shard_map/qhk,khd->qhd/dot_general | solution.py:73
  286.6 5.4 %copy.49 = f32[1024,1024]{1,0:T(8,128)} copy(f32[1024,1024]{0,1:T(8,128)} %bitcast.50) | data formatting | bytes 8388608 | tf_op jit(solution)/shard_map/reshape | solution.py:79
  292.0 9.3 %fusion.1 = f32[1024,16]{0,1:T(8,128)} fusion(f32[16,256,1024]{2,1,0:T(8,128)} %get-tuple-element.29, f32[1024,16]{0,1:T(8,128)S(1)} %copy-done.4), kind=kLoop, calls=%fused_computation.3 | loop fusion | flops 12566528 | bytes 16908288 | tf_op jit(solution)/shard_map/reduce_sum | solution.py:72
  301.3 144.6 %all-reduce.6.cloned.1.call-done = (f32[1024,16]{0,1:T(8,128)}, f32[1024,1024]{1,0:T(8,128)}) async-done(((f32[1024,16]{0,1:T(8,128)}, f32[1024,1024]{1,0:T(8,128)}), (f32[1024,16]{0,1:T(8,128)}, f32[1024,1024]{1,0:T(8,128)})) %all-reduce.6.cloned.1.call-update) | async-done | bytes 4259856 | tf_op jit(solution)/shard_map/psum | solution.py:81
  445.9 0.8 constant_dynamic-slice_fusion
  447.1 1.7 divide_convert_fusion.1
  (27 shorter events, 1.5 us)
Async XLA Ops:
  7.2 133.8 %copy-start = (bf16[1024,1024]{1,0:T(8,128)(2,1)S(1)}, bf16[1024,1024]{1,0:T(8,128)(2,1)}, u32[]{:S(2)}) copy-start(bf16[1024,1024]{1,0:T(8,128)(2,1)} %param.9) | copy-start | bytes 6291460
  7.2 67.2 %all-gather.2.cloned.1.call-start = ((), (), s32[]{:S(2)}) async-start(), calls=%async_computation.2 | async-start | bytes 6684672 | tf_op jit(solution)/shard_map/all_gather | solution.py:24
  122.5 2.7 copy-start.3
  125.2 15.8 %copy-start.1 = (bf16[256,1024]{1,0:T(8,128)(2,1)S(1)}, bf16[256,1024]{1,0:T(8,128)(2,1)}, u32[]{:S(2)}) copy-start(bf16[256,1024]{1,0:T(8,128)(2,1)} %param.7) | copy-start | bytes 1572868
  127.6 14.5 %copy-start.5 = (f32[1024]{0:T(1024)S(1)}, f32[1024]{0:T(1024)}, u32[]{:S(2)}) copy-start(f32[1024]{0:T(1024)} %param.12) | copy-start | bytes 12292
  127.6 14.5 %copy-start.6 = (f32[1024]{0:T(1024)S(1)}, f32[1024]{0:T(1024)}, u32[]{:S(2)}) copy-start(f32[1024]{0:T(1024)} %param.11) | copy-start | bytes 12292
  129.7 11.3 %all-to-all-start.1 = ((bf16[2,256,512]{1,2,0:T(8,128)(2,1)}), bf16[2,256,512]{1,2,0:T(8,128)(2,1)S(1)}, u32[]{:S(2)}, u32[]{:S(2)}) async-start(bf16[2,256,512]{1,2,0:T(8,128)(2,1)} %copy.44), calls=%async_computation.1 | async-start | bytes 1048576 | tf_op jit(solution)/shard_map/all_to_all | solution.py:55
  133.2 142.8 %all-reduce.4.cloned.1.call-start = ((), (), s32[]{:S(2)}) async-start(), calls=%async_computation.3 | async-start | bytes 131072 | tf_op jit(solution)/shard_map/pmax | solution.py:70
  142.3 4.5 copy-start.2
  158.5 287.4 %all-reduce.6.cloned.1.call-start = ((), (), s32[]{:S(2)}) async-start(), calls=%async_computation.4 | async-start | bytes 8519680 | tf_op jit(solution)/shard_map/psum | solution.py:81
  286.6 5.4 %copy-start.4 = (f32[1024,16]{0,1:T(8,128)S(1)}, f32[1024,16]{0,1:T(8,128)}, u32[]{:S(2)}) copy-start(f32[1024,16]{0,1:T(8,128)} %all-reduce.4.cloned.1.call-done) | copy-start | bytes 196612
Sparse Core Ops, SparseCore 0:
  10.3 64.1 all-gather.1
  158.6 117.3 all-reduce.3
  301.4 144.3 all-reduce.5
where the time goes:
time: 456 us; the launch traced here: 455 us
  waiting for transfers between devices  333 us (73%)
  matrix products  35.1 us (8%)
  local copies, waits for them, and re-layouts  29 us (6%)
  blocking collectives  28.1 us (6%)
  between operations  13.9 us (3%)
  other arithmetic  12.8 us (3%)
    psum x1, waiting for transfers between devices, per_device(): summed, sum_total = lax.psum((numerator, cross_total), ('span', 'seq'))  145 us
    pmax x1, waiting for transfers between devices, per_device(): cross_peak = lax.pmax(local_peak, ('span', 'seq'))  117 us
    all_gather x1, waiting for transfers between devices, per_device(): lax.all_gather(w_qkv, 'span', axis=0, tiled=True)  66.5 us
    all_to_all x1, blocking collectives, per_device(): lax.all_to_all(projected, 'seq', split_axis=2, concat_axis=0, tiled=True)  28.1 us
    dot_general x1, matrix products, per_device(): jnp.einsum('qhk,khd->qhd', cross_powers.astype(jnp.bfloat16), cross_value...  10.7 us
    dot_general x1, matrix products, per_device(): jnp.einsum('qhd,khd->qhk', query_heads, cross_keys, preferred_element_typ...  10.3 us
    reduce_sum x1, other arithmetic, per_device(): cross_total = jnp.sum(cross_powers, -1)  9.28 us
  transfers between devices with their start and end apart: 4, of which 4 were waited for; matrix products, arithmetic and copies ran while one was open for 1% of the time, Pallas kernels for 0%

commit v1 on v0

--- a/solution.py
+++ b/solution.py
@@ -6,6 +6,19 @@
 H = 16
 DH = 64
 score_scale = 0.125
+
+
+def gather_around(shard, axis, dim):
+    ways = lax.axis_size(axis)
+    up = [(d, (d + 1) % ways) for d in range(ways)]
+    down = [(d, (d - 1) % ways) for d in range(ways)]
+    earlier, later = ([shard], [shard])
+    for _ in range(ways // 2):
+        earlier.append(lax.ppermute(earlier[-1], axis, up))
+    for _ in range((ways - 1) // 2):
+        later.append(lax.ppermute(later[-1], axis, down))
+    line = jnp.concatenate([*earlier[::-1], *later[1:]], axis=dim)
+    return jnp.roll(line, (lax.axis_index(axis) - ways // 2) * shard.shape[dim], axis=dim)
 
 
 def layer_norm(residual, ln_gain, ln_bias):
@@ -19,11 +32,7 @@
     model_width = tokens.shape[1]
     seq_count = lax.axis_size("seq")
     span_count = lax.axis_size("span")
-    projected = jnp.dot(
-        tokens,
-        lax.all_gather(w_qkv, "span", axis=0, tiled=True),
-        preferred_element_type=jnp.float32,
-    )
+    projected = jnp.dot(tokens, gather_around(w_qkv, "span", 0), preferred_element_type=jnp.float32)
     projected = projected.astype(jnp.bfloat16).reshape(tok_rows, 3, model_width)
     grouped = lax.all_to_all(projected, "seq", split_axis=2, concat_axis=0, tiled=True)
     span_length = tok_rows * seq_count

time: 456 us -> 478 us (1.048)
  starting transfers between devices: 3.79 us -> 38.1 us
  waiting for transfers between devices: 333 us -> 309 us
  local copies, waits for them, and re-layouts: 29 us -> 43.2 us
    all_gather x1 -> x0, waiting for transfers between devices: 66.5 us -> none  [per_device(): lax.all_gather(w_qkv, 'span', axis=0, tiled=True)]
    ppermute x0 -> x15, waiting for transfers between devices: none -> 46.4 us  [the longest x8 46 us: gather_around(): earlier.append(lax.ppermute(earlier[-1], axis, up))]
    ppermute x0 -> x15, starting transfers between devices: none -> 34.3 us  [the longest x7 30.9 us: gather_around(): later.append(lax.ppermute(later[-1], axis, down))]
    unnamed x15 -> x80, local copies, waits for them, and re-layouts: 4 us -> 22.6 us
  transfers between devices with their start and end apart: 4 -> 18, of which waited for: 4 -> 12; matrix products, arithmetic and copies ran while one was open for 1% -> 4% of each run, Pallas kernels for 0% -> 0%
where the time goes in v1:
time: 478 us; the launch traced here: 477 us
  waiting for transfers between devices  309 us (65%)
  local copies, waits for them, and re-layouts  43.2 us (9%)
  starting transfers between devices  38.1 us (8%)
  matrix products  31.1 us (7%)
  blocking collectives  27.8 us (6%)
  between operations  14.5 us (3%)
  other arithmetic  12.8 us (3%)
    psum x1, waiting for transfers between devices, per_device(): summed, sum_total = lax.psum((numerator, cross_total), ('span', 'seq'))  145 us
    pmax x1, waiting for transfers between devices, per_device(): cross_peak = lax.pmax(local_peak, ('span', 'seq'))  115 us
    ppermute x8, waiting for transfers between devices, gather_around(): earlier.append(lax.ppermute(earlier[-1], axis, up))  46 us
    ppermute x7, starting transfers between devices, gather_around(): later.append(lax.ppermute(later[-1], axis, down))  30.9 us
    all_to_all x1, blocking collectives, per_device(): lax.all_to_all(projected, 'seq', split_axis=2, concat_axis=0, tiled=True)  27.8 us
    unnamed x80, local copies, waits for them, and re-layouts  22.6 us
    dot_general x1, matrix products, per_device(): jnp.einsum('qhk,khd->qhd', cross_powers.astype(jnp.bfloat16), cross_value...  10.8 us
    dot_general x1, matrix products, per_device(): jnp.einsum('qhd,khd->qhk', query_heads, cross_keys, preferred_element_typ...  10.3 us
  transfers between devices with their start and end apart: 18, of which 12 were waited for; matrix products, arithmetic and copies ran while one was open for 4% of the time, Pallas kernels for 0%

profile of v1, /device:TPU:0, one launch (start us, length us, event | category | flops | bytes accessed | tf_op | source)
XLA Modules:
  0.0 476.9 jit_solution(130620742023209305)
XLA Ops:
  7.7 10.6 %collective-permute-done = bf16[64,3072]{1,0:T(8,128)(2,1)S(1)} collective-permute-done((bf16[64,3072]{1,0:T(8,128)(2,1)}, bf16[64,3072]{1,0:T(8,128)(2,1)S(1)}, u32[]{:S(2)}, u32[]{:S(2)}) %collective-permute-start) | collective-permute-done | bytes 393248 | tf_op jit(solution)/shard_map/ppermute | solution.py:17
  18.4 4.4 collective-permute-start.8
  22.8 5.6 %collective-permute-done.1 = bf16[64,3072]{1,0:T(8,128)(2,1)S(1)} collective-permute-done((bf16[64,3072]{1,0:T(8,128)(2,1)S(1)}, bf16[64,3072]{1,0:T(8,128)(2,1)S(1)}, u32[]{:S(2)}, u32[]{:S(2)}) %collective-permute-start.1) | collective-permute-done | bytes 393248 | tf_op jit(solution)/shard_map/ppermute | solution.py:17
  28.4 4.6 collective-permute-start.9
  33.0 5.3 %collective-permute-done.2 = bf16[64,3072]{1,0:T(8,128)(2,1)S(1)} collective-permute-done((bf16[64,3072]{1,0:T(8,128)(2,1)S(1)}, bf16[64,3072]{1,0:T(8,128)(2,1)S(1)}, u32[]{:S(2)}, u32[]{:S(2)}) %collective-permute-start.2) | collective-permute-done | bytes 393248 | tf_op jit(solution)/shard_map/ppermute | solution.py:17
  38.4 4.6 collective-permute-start.10
  43.0 5.3 %collective-permute-done.3 = bf16[64,3072]{1,0:T(8,128)(2,1)S(1)} collective-permute-done((bf16[64,3072]{1,0:T(8,128)(2,1)S(1)}, bf16[64,3072]{1,0:T(8,128)(2,1)S(1)}, u32[]{:S(2)}, u32[]{:S(2)}) %collective-permute-start.3) | collective-permute-done | bytes 393248 | tf_op jit(solution)/shard_map/ppermute | solution.py:17
  48.8 4.2 collective-permute-start.11
  53.0 5.4 %collective-permute-done.4 = bf16[64,3072]{1,0:T(8,128)(2,1)S(1)} collective-permute-done((bf16[64,3072]{1,0:T(8,128)(2,1)S(1)}, bf16[64,3072]{1,0:T(8,128)(2,1)S(1)}, u32[]{:S(2)}, u32[]{:S(2)}) %collective-permute-start.4) | collective-permute-done | bytes 393248 | tf_op jit(solution)/shard_map/ppermute | solution.py:17
  60.3 3.5 collective-permute-start.12
  63.8 4.6 collective-permute-done.5
  69.1 4.8 %collective-permute-start.13 = (bf16[64,3072]{1,0:T(8,128)(2,1)}, bf16[64,3072]{1,0:T(8,128)(2,1)}, u32[]{:S(2)}, u32[]{:S(2)}) collective-permute-start(bf16[64,3072]{1,0:T(8,128)(2,1)} %collective-permute-done.12), channel_id=1, source_target_pairs={{0,30},{2,0},{4,2},{6,4},{8,6},{10,8},{12,10},{14,12},{16,14},{18,... | collective-permute-start | bytes 1179656 | tf_op jit(solution)/shard_map/ppermute | solution.py:19
  73.9 4.6 collective-permute-done.6
  79.5 4.7 collective-permute-start.14
  84.2 4.6 collective-permute-done.7
  106.9 1.9 fusion.15
  110.2 27.8 %all_to_all.37 = bf16[256,3,1024]{0,1,2:T(4,128)(2,1)S(1)} all-to-all(bf16[256,3,1024]{0,1,2:T(4,128)(2,1)S(1)} %copy.24), channel_id=1, replica_groups=mesh['span'=16,'seq'=2] {'seq'}, dimensions={2} | all-to-all | bytes 3145728 | tf_op jit(solution)/shard_map/all_to_all | solution.py:37
  138.0 3.1 copy.25
  141.1 3.7 all_to_all.30
  144.8 1.5 fusion.26
  149.0 2.4 divide_convert_fusion
  153.4 3.5 all-to-all-start.1
  157.0 3.9 copy.30
  160.9 3.1 all-to-all-done.1
  165.4 3.7 convolution_convert_fusion
  171.2 10.3 %bitcast_reduce_fusion = (f32[1024,16]{0,1:T(8,128)}, f32[16,256,1024]{2,1,0:T(8,128)}) fusion(bf16[256,16,64]{0,2,1:T(8,128)(2,1)S(1)} %bitcast.56, bf16[1024,16,64]{0,2,1:T(8,128)(2,1)} %bitcast.53), kind=kOutput, calls=%fused_computation.1 | convolution fusion | flops 545243136 | bytes 19464192 | tf_op jit(solution)/shard_map/qhd,khd->qhk/dot_general | solution.py:75
  182.0 115.3 %all-reduce.4.cloned.1.call-done = f32[1024,16]{0,1:T(8,128)} async-done(((f32[1024,16]{0,1:T(8,128)}), f32[1024,16]{0,1:T(8,128)}) %all-reduce.4.cloned.1.call-update) | async-done | bytes 65552 | tf_op jit(solution)/shard_map/pmax | solution.py:79
  297.2 10.8 %fusion.3 = f32[16,64,1024]{2,1,0:T(8,128)} fusion(bf16[256,16,64]{0,2,1:T(8,128)(2,1)S(1)} %bitcast.59, f32[16,256,1024]{2,1,0:T(8,128)} %get-tuple-element.29, f32[1024,16]{0,1:T(8,128)} %all-reduce.4.cloned.1.call-done), kind=kOutput, calls=%fused_computation.5 | convolution fusion | flops 549453824 | bytes 21561344 | tf_op jit(solution)/shard_map/qhk,khd->qhd/dot_general | solution.py:82
  308.0 5.3 %copy.32 = f32[1024,1024]{1,0:T(8,128)} copy(f32[1024,1024]{0,1:T(8,128)} %bitcast.52) | data formatting | bytes 8388608 | tf_op jit(solution)/shard_map/reshape | solution.py:88
  313.3 9.3 %fusion.1 = f32[1024,16]{0,1:T(8,128)} fusion(f32[16,256,1024]{2,1,0:T(8,128)} %get-tuple-element.29, f32[1024,16]{0,1:T(8,128)S(1)} %copy-done.21), kind=kLoop, calls=%fused_computation.3 | loop fusion | flops 12566528 | bytes 16908288 | tf_op jit(solution)/shard_map/reduce_sum | solution.py:81
  322.7 144.6 %all-reduce.6.cloned.1.call-done = (f32[1024,16]{0,1:T(8,128)}, f32[1024,1024]{1,0:T(8,128)}) async-done(((f32[1024,16]{0,1:T(8,128)}, f32[1024,1024]{1,0:T(8,128)}), (f32[1024,16]{0,1:T(8,128)}, f32[1024,1024]{1,0:T(8,128)})) %all-reduce.6.cloned.1.call-update) | async-done | bytes 4259856 | tf_op jit(solution)/shard_map/psum | solution.py:90
  468.4 1.7 divide_convert_fusion.1
  (116 shorter events, 33.9 us)
Async XLA Ops:
  7.2 156.8 %copy-start = (bf16[1024,1024]{1,0:T(8,128)(2,1)S(1)}, bf16[1024,1024]{1,0:T(8,128)(2,1)}, u32[]{:S(2)}) copy-start(bf16[1024,1024]{1,0:T(8,128)(2,1)} %param.9) | copy-start | bytes 6291460
  7.2 97.4 %copy-start.1 = (bf16[64,3072]{1,0:T(8,128)(2,1)S(1)}, bf16[64,3072]{1,0:T(8,128)(2,1)}, u32[]{:S(2)}) copy-start(bf16[64,3072]{1,0:T(8,128)(2,1)} %param.8) | copy-start | bytes 1179652
  7.2 11.2 %collective-permute-start = (bf16[64,3072]{1,0:T(8,128)(2,1)}, bf16[64,3072]{1,0:T(8,128)(2,1)S(1)}, u32[]{:S(2)}, u32[]{:S(2)}) collective-permute-start(bf16[64,3072]{1,0:T(8,128)(2,1)} %param.8), channel_id=1, source_target_pairs={{0,2},{2,4},{4,6},{6,8},{8,10},{10,12},{12,14},{14,16},{16,18},{18... | collective-permute-start | bytes 1179656 | tf_op jit(solution)/shard_map/ppermute | solution.py:17
  18.4 10.0 %collective-permute-start.1 = (bf16[64,3072]{1,0:T(8,128)(2,1)S(1)}, bf16[64,3072]{1,0:T(8,128)(2,1)S(1)}, u32[]{:S(2)}, u32[]{:S(2)}) collective-permute-start(bf16[64,3072]{1,0:T(8,128)(2,1)S(1)} %collective-permute-done), channel_id=1, source_target_pairs={{0,2},{2,4},{4,6},{6,8},{8,10},{10,12},{12,14},{14,16},{16,18},{18... | collective-permute-start | bytes 1179656 | tf_op jit(solution)/shard_map/ppermute | solution.py:17
  18.4 10.1 %collective-permute-start.8 = (bf16[64,3072]{1,0:T(8,128)(2,1)}, bf16[64,3072]{1,0:T(8,128)(2,1)S(1)}, u32[]{:S(2)}, u32[]{:S(2)}) collective-permute-start(bf16[64,3072]{1,0:T(8,128)(2,1)} %param.8), channel_id=1, source_target_pairs={{0,30},{2,0},{4,2},{6,4},{8,6},{10,8},{12,10},{14,12},{16,14},{18,... | collective-permute-start | bytes 1179656 | tf_op jit(solution)/shard_map/ppermute | solution.py:19
  28.4 10.0 %collective-permute-start.2 = (bf16[64,3072]{1,0:T(8,128)(2,1)S(1)}, bf16[64,3072]{1,0:T(8,128)(2,1)S(1)}, u32[]{:S(2)}, u32[]{:S(2)}) collective-permute-start(bf16[64,3072]{1,0:T(8,128)(2,1)S(1)} %collective-permute-done.1), channel_id=1, source_target_pairs={{0,2},{2,4},{4,6},{6,8},{8,10},{10,12},{12,14},{14,16},{16,18},{18... | collective-permute-start | bytes 1179656 | tf_op jit(solution)/shard_map/ppermute | solution.py:17
  28.4 10.0 %collective-permute-start.9 = (bf16[64,3072]{1,0:T(8,128)(2,1)S(1)}, bf16[64,3072]{1,0:T(8,128)(2,1)S(1)}, u32[]{:S(2)}, u32[]{:S(2)}) collective-permute-start(bf16[64,3072]{1,0:T(8,128)(2,1)S(1)} %collective-permute-done.8), channel_id=1, source_target_pairs={{0,30},{2,0},{4,2},{6,4},{8,6},{10,8},{12,10},{14,12},{16,14},{18,... | collective-permute-start | bytes 1179656 | tf_op jit(solution)/shard_map/ppermute | solution.py:19
  38.4 10.0 %collective-permute-start.3 = (bf16[64,3072]{1,0:T(8,128)(2,1)S(1)}, bf16[64,3072]{1,0:T(8,128)(2,1)S(1)}, u32[]{:S(2)}, u32[]{:S(2)}) collective-permute-start(bf16[64,3072]{1,0:T(8,128)(2,1)S(1)} %collective-permute-done.2), channel_id=1, source_target_pairs={{0,2},{2,4},{4,6},{6,8},{8,10},{10,12},{12,14},{14,16},{16,18},{18... | collective-permute-start | bytes 1179656 | tf_op jit(solution)/shard_map/ppermute | solution.py:17
  38.4 10.4 %collective-permute-start.10 = (bf16[64,3072]{1,0:T(8,128)(2,1)S(1)}, bf16[64,3072]{1,0:T(8,128)(2,1)S(1)}, u32[]{:S(2)}, u32[]{:S(2)}) collective-permute-start(bf16[64,3072]{1,0:T(8,128)(2,1)S(1)} %collective-permute-done.9), channel_id=1, source_target_pairs={{0,30},{2,0},{4,2},{6,4},{8,6},{10,8},{12,10},{14,12},{16,14},{18,... | collective-permute-start | bytes 1179656 | tf_op jit(solution)/shard_map/ppermute | solution.py:19
  48.4 20.7 %copy-start.12 = (bf16[64,3072]{1,0:T(8,128)(2,1)}, bf16[64,3072]{1,0:T(8,128)(2,1)S(1)}, u32[]{:S(2)}) copy-start(bf16[64,3072]{1,0:T(8,128)(2,1)S(1)} %collective-permute-done.3) | copy-start | bytes 1179652
  48.4 10.0 %collective-permute-start.4 = (bf16[64,3072]{1,0:T(8,128)(2,1)S(1)}, bf16[64,3072]{1,0:T(8,128)(2,1)S(1)}, u32[]{:S(2)}, u32[]{:S(2)}) collective-permute-start(bf16[64,3072]{1,0:T(8,128)(2,1)S(1)} %collective-permute-done.3), channel_id=1, source_target_pairs={{0,2},{2,4},{4,6},{6,8},{8,10},{10,12},{12,14},{14,16},{16,18},{18... | collective-permute-start | bytes 1179656 | tf_op jit(solution)/shard_map/ppermute | solution.py:17
  48.8 10.7 %collective-permute-start.11 = (bf16[64,3072]{1,0:T(8,128)(2,1)S(1)}, bf16[64,3072]{1,0:T(8,128)(2,1)S(1)}, u32[]{:S(2)}, u32[]{:S(2)}) collective-permute-start(bf16[64,3072]{1,0:T(8,128)(2,1)S(1)} %collective-permute-done.10), channel_id=1, source_target_pairs={{0,30},{2,0},{4,2},{6,4},{8,6},{10,8},{12,10},{14,12},{16,14},{18,... | collective-permute-start | bytes 1179656 | tf_op jit(solution)/shard_map/ppermute | solution.py:19
  58.4 10.0 %collective-permute-start.5 = (bf16[64,3072]{1,0:T(8,128)(2,1)S(1)}, bf16[64,3072]{1,0:T(8,128)(2,1)S(1)}, u32[]{:S(2)}, u32[]{:S(2)}) collective-permute-start(bf16[64,3072]{1,0:T(8,128)(2,1)S(1)} %collective-permute-done.4), channel_id=1, source_target_pairs={{0,2},{2,4},{4,6},{6,8},{8,10},{10,12},{12,14},{14,16},{16,18},{18... | collective-permute-start | bytes 1179656 | tf_op jit(solution)/shard_map/ppermute | solution.py:17
  60.3 8.8 %collective-permute-start.12 = (bf16[64,3072]{1,0:T(8,128)(2,1)S(1)}, bf16[64,3072]{1,0:T(8,128)(2,1)}, u32[]{:S(2)}, u32[]{:S(2)}) collective-permute-start(bf16[64,3072]{1,0:T(8,128)(2,1)S(1)} %collective-permute-done.11), channel_id=1, source_target_pairs={{0,30},{2,0},{4,2},{6,4},{8,6},{10,8},{12,10},{14,12},{16,14},{18,... | collective-permute-start | bytes 1179656 | tf_op jit(solution)/shard_map/ppermute | solution.py:19
  68.4 10.1 %collective-permute-start.6 = (bf16[64,3072]{1,0:T(8,128)(2,1)S(1)}, bf16[64,3072]{1,0:T(8,128)(2,1)}, u32[]{:S(2)}, u32[]{:S(2)}) collective-permute-start(bf16[64,3072]{1,0:T(8,128)(2,1)S(1)} %collective-permute-done.5), channel_id=1, source_target_pairs={{0,2},{2,4},{4,6},{6,8},{8,10},{10,12},{12,14},{14,16},{16,18},{18... | collective-permute-start | bytes 1179656 | tf_op jit(solution)/shard_map/ppermute | solution.py:17
  69.1 10.4 %collective-permute-start.13 = (bf16[64,3072]{1,0:T(8,128)(2,1)}, bf16[64,3072]{1,0:T(8,128)(2,1)}, u32[]{:S(2)}, u32[]{:S(2)}) collective-permute-start(bf16[64,3072]{1,0:T(8,128)(2,1)} %collective-permute-done.12), channel_id=1, source_target_pairs={{0,30},{2,0},{4,2},{6,4},{8,6},{10,8},{12,10},{14,12},{16,14},{18,... | collective-permute-start | bytes 1179656 | tf_op jit(solution)/shard_map/ppermute | solution.py:19
  78.5 10.3 %collective-permute-start.7 = (bf16[64,3072]{1,0:T(8,128)(2,1)}, bf16[64,3072]{1,0:T(8,128)(2,1)}, u32[]{:S(2)}, u32[]{:S(2)}) collective-permute-start(bf16[64,3072]{1,0:T(8,128)(2,1)} %collective-permute-done.6), channel_id=1, source_target_pairs={{0,2},{2,4},{4,6},{6,8},{8,10},{10,12},{12,14},{14,16},{16,18},{18... | collective-permute-start | bytes 1179656 | tf_op jit(solution)/shard_map/ppermute | solution.py:17
  79.1 25.2 %copy-start.17 = (bf16[64,3072]{1,0:T(8,128)(2,1)S(1)}, bf16[64,3072]{1,0:T(8,128)(2,1)}, u32[]{:S(2)}) copy-start(bf16[64,3072]{1,0:T(8,128)(2,1)} %copy-done.16) | copy-start | bytes 1179652
  79.1 25.3 %copy-start.15 = (bf16[64,3072]{1,0:T(8,128)(2,1)S(1)}, bf16[64,3072]{1,0:T(8,128)(2,1)}, u32[]{:S(2)}) copy-start(bf16[64,3072]{1,0:T(8,128)(2,1)} %copy-done.14) | copy-start | bytes 1179652
  79.1 25.3 %copy-start.13 = (bf16[64,3072]{1,0:T(8,128)(2,1)S(1)}, bf16[64,3072]{1,0:T(8,128)(2,1)}, u32[]{:S(2)}) copy-start(bf16[64,3072]{1,0:T(8,128)(2,1)} %copy-done.12) | copy-start | bytes 1179652
  79.1 25.4 %copy-start.7 = (bf16[64,3072]{1,0:T(8,128)(2,1)S(1)}, bf16[64,3072]{1,0:T(8,128)(2,1)}, u32[]{:S(2)}) copy-start(bf16[64,3072]{1,0:T(8,128)(2,1)} %copy-done.6) | copy-start | bytes 1179652
  79.1 25.4 %copy-start.3 = (bf16[64,3072]{1,0:T(8,128)(2,1)S(1)}, bf16[64,3072]{1,0:T(8,128)(2,1)}, u32[]{:S(2)}) copy-start(bf16[64,3072]{1,0:T(8,128)(2,1)} %copy-done.2) | copy-start | bytes 1179652
  79.1 25.6 %copy-start.5 = (bf16[64,3072]{1,0:T(8,128)(2,1)S(1)}, bf16[64,3072]{1,0:T(8,128)(2,1)}, u32[]{:S(2)}) copy-start(bf16[64,3072]{1,0:T(8,128)(2,1)} %copy-done.4) | copy-start | bytes 1179652
  79.1 25.6 %copy-start.9 = (bf16[64,3072]{1,0:T(8,128)(2,1)S(1)}, bf16[64,3072]{1,0:T(8,128)(2,1)}, u32[]{:S(2)}) copy-start(bf16[64,3072]{1,0:T(8,128)(2,1)} %copy-done.8) | copy-start | bytes 1179652
  79.1 25.6 %copy-start.11 = (bf16[64,3072]{1,0:T(8,128)(2,1)S(1)}, bf16[64,3072]{1,0:T(8,128)(2,1)}, u32[]{:S(2)}) copy-start(bf16[64,3072]{1,0:T(8,128)(2,1)} %copy-done.10) | copy-start | bytes 1179652
  79.1 27.8 %copy-start.18 = (bf16[256,1024]{1,0:T(8,128)(2,1)S(1)}, bf16[256,1024]{1,0:T(8,128)(2,1)}, u32[]{:S(2)}) copy-start(bf16[256,1024]{1,0:T(8,128)(2,1)} %param.7) | copy-start | bytes 1572868
  79.5 22.7 %collective-permute-start.14 = (bf16[64,3072]{1,0:T(8,128)(2,1)}, bf16[64,3072]{1,0:T(8,128)(2,1)S(1)}, u32[]{:S(2)}, u32[]{:S(2)}) collective-permute-start(bf16[64,3072]{1,0:T(8,128)(2,1)} %collective-permute-done.13), channel_id=1, source_target_pairs={{0,30},{2,0},{4,2},{6,4},{8,6},{10,8},{12,10},{14,12},{16,14},{18,... | collective-permute-start | bytes 1179656 | tf_op jit(solution)/shard_map/ppermute | solution.py:19
  147.6 16.4 %copy-start.19 = (bf16[256,1024]{1,0:T(8,128)(2,1)S(1)}, bf16[256,1024]{1,0:T(8,128)(2,1)}, u32[]{:S(2)}) copy-start(bf16[256,1024]{1,0:T(8,128)(2,1)} %param.7) | copy-start | bytes 1572868
  153.4 10.5 %all-to-all-start.1 = ((bf16[2,256,512]{1,2,0:T(8,128)(2,1)}), bf16[2,256,512]{1,2,0:T(8,128)(2,1)S(1)}, u32[]{:S(2)}, u32[]{:S(2)}) async-start(bf16[2,256,512]{1,2,0:T(8,128)(2,1)} %copy.27), calls=%async_computation.1 | async-start | bytes 1048576 | tf_op jit(solution)/shard_map/all_to_all | solution.py:64
  156.9 140.3 %all-reduce.4.cloned.1.call-start = ((), (), s32[]{:S(2)}) async-start(), calls=%async_computation.2 | async-start | bytes 131072 | tf_op jit(solution)/shard_map/pmax | solution.py:79
  181.5 285.7 %all-reduce.6.cloned.1.call-start = ((), (), s32[]{:S(2)}) async-start(), calls=%async_computation.3 | async-start | bytes 8519680 | tf_op jit(solution)/shard_map/psum | solution.py:90
  297.2 16.1 %copy-start.21 = (f32[1024,16]{0,1:T(8,128)S(1)}, f32[1024,16]{0,1:T(8,128)}, u32[]{:S(2)}) copy-start(f32[1024,16]{0,1:T(8,128)} %all-reduce.4.cloned.1.call-done) | copy-start | bytes 196612
  (10 other events, 92.5 us)
Sparse Core Ops, SparseCore 0:
  181.6 115.5 all-reduce.3
  322.8 144.3 all-reduce.5
